TPU v7x, 32 devices: a whole 2x2x4 slice. The times are simulated.
32 devices in a mesh: fsdp: 8 (over y, x, core), seq: 4 (over z).
Axes of the slice: x: 2, y: 2, z: 4, core: 2. Of those that a mesh axis runs over, the one named last changes fastest.
Arguments:
- latents_in: bfloat16 [2, 8, 128, 768], P(None, 'fsdp'), may hold values from -6 to 6
- inputs: bfloat16 [2, 8, 6312, 768], P(None, 'fsdp', 'seq'), may hold values from -6 to 6
- clip_frames: int32 [2, 8], P(None, 'fsdp'), may hold values from 4 to 16
- text_mask: int32 [2, 8, 40], P(None, 'fsdp'), may hold values 0 or 1
- qkv_weight: bfloat16 [2, 3, 768, 768], P(None, None, 'fsdp'), may hold values from -0.21875 to 0.21875
- out_weight: bfloat16 [2, 768, 768], P(None, 'fsdp'), may hold values from -1.75 to 1.75
- mlp_in: bfloat16 [2, 768, 3072], P(None, 'fsdp'), may hold values from -0.21875 to 0.21875
- mlp_out: bfloat16 [2, 3072, 768], P(None, 'fsdp'), may hold values from -0.109375 to 0.109375
- norm_gain: bfloat16 [5, 768], P(None, 'fsdp'), may hold values from 0.5 to 1.5
- norm_bias: bfloat16 [5, 768], P(None, 'fsdp'), may hold values from -2.5 to 2.5
- bias_in: bfloat16 [2, 3072], P(None, 'fsdp'), may hold values from -2.5 to 2.5
- bias_out: bfloat16 [2, 768], P(None, 'fsdp'), may hold values from -2.5 to 2.5
- out_cotangent: bfloat16 [2, 8, 128, 768], P(None, 'fsdp'), may hold values from -6 to 6
Outputs:
- latents_out: float32 [2, 8, 128, 768], P(None, 'fsdp')
- latents_grad: float32 [2, 8, 128, 768], P(None, 'fsdp')
- inputs_grad: float32 [2, 8, 6312, 768], P(None, 'fsdp', 'seq')
- qkv_grad: float32 [2, 3, 768, 768], P(None, None, 'fsdp')
- out_weight_grad: float32 [2, 768, 768], P(None, 'fsdp')
- mlp_in_grad: float32 [2, 768, 3072], P(None, 'fsdp')
- mlp_out_grad: float32 [2, 3072, 768], P(None, 'fsdp')
- norm_gain_grad: float32 [5, 768], P(None, 'fsdp')
- norm_bias_grad: float32 [5, 768], P(None, 'fsdp')
- bias_in_grad: float32 [2, 3072], P(None, 'fsdp')
- bias_out_grad: float32 [2, 768], P(None, 'fsdp')
Inputs may be any that keep to these rules, and one draw needn't show every extreme that they name: `clip_frames`: frames of each clip; its first 392 times that many patch slots hold tokens, the rest of its 16 frame slots are padding.
All inputs are finite; a program needn't handle non-finite values. No bound on the sum of `text_mask` on one device may be relied on, other than what follows from the above.
Results may differ from a plain program's by a relative error of at most 0.015.
Values may be sent and summed in bfloat16 or wider, within the bound.
No kernel may reach another device: no remote copies, remote signals or barrier semaphores. Data moves between devices by JAX's collectives and lax.ppermute only.
A program may use at most 320 MiB of HBM per device.

v0:
```python
import jax
import jax.numpy as jnp
from jax import lax
from jax.sharding import PartitionSpec as P

D = 768
HEADS = 12
HEAD = 64
PATCHES = 392
FRAMES = 16
epsilon = 1e-06


def layer_norm(values, scales, offsets):
    center = values - jnp.mean(values, -1, keepdims=True)
    spread = jnp.mean(center * center, -1, keepdims=True)
    return center * lax.rsqrt(spread + epsilon) * scales + offsets


def to_half(values):
    return values.astype(jnp.bfloat16)


def product(form, left, right):
    return jnp.einsum(form, left, right, preferred_element_type=jnp.float32)


def norm_back(values, scales, offsets, grad_normed):
    unused, pullback = jax.vjp(layer_norm, values, scales, offsets)
    return pullback(grad_normed)


def feed_forward(residual, up_w, down_w, up_b, down_b, scales, offsets):
    normed = to_half(layer_norm(residual, scales, offsets))
    hidden = product("cnd,df->cnf", normed, up_w) + up_b
    active = to_half(jax.nn.gelu(hidden))
    result = product("cnf,fd->cnd", active, down_w) + down_b
    return (result, (residual, normed, hidden, active))


def feed_back(stored, grad_in, up_w, down_w, scales, offsets):
    residual, normed, hidden, active = stored
    grad_y = to_half(grad_in)
    grad_down = product("cnf,cnd->fd", active, grad_y)
    grad_down_b = jnp.sum(grad_y, (0, 1), dtype=jnp.float32)
    grad_act = product("cnd,fd->cnf", grad_y, down_w)
    unused, gelu_pull = jax.vjp(jax.nn.gelu, hidden)
    grad_hidden = to_half(gelu_pull(grad_act)[0])
    grad_up = product("cnd,cnf->df", normed, grad_hidden)
    grad_up_b = jnp.sum(grad_hidden, (0, 1), dtype=jnp.float32)
    grad_normed = product("cnf,df->cnd", grad_hidden, up_w)
    grad_rows, grad_scales, grad_offsets = norm_back(residual, scales, offsets, grad_normed)
    return (grad_rows, (grad_up, grad_down, grad_up_b, grad_down_b, grad_scales, grad_offsets))


def self_forward(residual, qkv_w, out_w, scales, offsets):
    clip_count, latent_count = (residual.shape[0], residual.shape[1])
    normed = to_half(layer_norm(residual, scales, offsets))
    heads_qkv = to_half(product("cnd,jde->jcne", normed, qkv_w)).reshape(
        3, clip_count, latent_count, HEADS, HEAD
    )
    scores = product("cqhd,ckhd->cqhk", heads_qkv[0], heads_qkv[1]) * 0.125
    row_peak = jnp.max(scores, -1, keepdims=True)
    self_exp = jnp.exp(scores - row_peak)
    softmax_w = self_exp / jnp.sum(self_exp, -1, keepdims=True)
    mixed_heads = to_half(product("cqhk,ckhd->cqhd", to_half(softmax_w), heads_qkv[2])).reshape(
        clip_count, latent_count, D
    )
    result = product("cnd,de->cne", mixed_heads, out_w)
    return (result, (residual, normed, heads_qkv, softmax_w, mixed_heads))


def self_back(stored, grad_in, qkv_w, out_w, scales, offsets):
    residual, normed, heads_qkv, softmax_w, mixed_heads = stored
    clip_count, latent_count = (residual.shape[0], residual.shape[1])
    grad_a = to_half(grad_in)
    grad_out_w = product("cnd,cne->de", mixed_heads, grad_a)
    grad_mixed = to_half(product("cne,de->cnd", grad_a, out_w)).reshape(
        clip_count, latent_count, HEADS, HEAD
    )
    grad_probs = product("cqhd,ckhd->cqhk", grad_mixed, heads_qkv[2])
    grad_values = to_half(product("cqhk,cqhd->ckhd", to_half(softmax_w), grad_mixed))
    grad_scores = to_half(
        softmax_w * (grad_probs - jnp.sum(softmax_w * grad_probs, -1, keepdims=True))
    )
    grad_queries = to_half(product("cqhk,ckhd->cqhd", grad_scores, heads_qkv[1]) * 0.125)
    grad_keys = to_half(product("cqhk,cqhd->ckhd", grad_scores, heads_qkv[0]) * 0.125)
    stacked = jnp.stack([grad_queries, grad_keys, grad_values]).reshape(
        3, clip_count, latent_count, D
    )
    grad_qkv = product("cnd,jcne->jde", normed, stacked)
    grad_normed = product("jcne,jde->cnd", stacked, qkv_w)
    grad_rows, grad_scales, grad_offsets = norm_back(residual, scales, offsets, grad_normed)
    return (grad_rows, (grad_qkv, grad_out_w, grad_scales, grad_offsets))


def cross_scores(queries, key_heads, valid_keys):
    scores = product("cqhd,ckhd->cqhk", queries, key_heads) * 0.125
    return jnp.where(valid_keys[:, None, None, :], jnp.exp(scores), 0.0)


def cross_forward(residual, tokens, valid_keys, qkv_w, out_w, scales, offsets):
    clip_count, latent_count, local_len = (residual.shape[0], residual.shape[1], tokens.shape[1])
    latent_normed = to_half(layer_norm(residual, scales[0], offsets[0]))
    token_normed = to_half(layer_norm(tokens, scales[1], offsets[1]))
    queries = to_half(product("cnd,de->cne", latent_normed, qkv_w[0])).reshape(
        clip_count, latent_count, HEADS, HEAD
    )
    keyval = to_half(product("cld,jde->jcle", token_normed, qkv_w[1:3])).reshape(
        2, clip_count, local_len, HEADS, HEAD
    )
    weights_exp = cross_scores(queries, keyval[0], valid_keys)
    numer_part = product("cqhk,ckhd->cqhd", to_half(weights_exp), keyval[1])
    numer_share, total_share = (
        lax.psum_scatter(numer_part, "seq", scatter_dimension=2, tiled=True),
        lax.psum_scatter(jnp.sum(weights_exp, -1), "seq", scatter_dimension=2, tiled=True),
    )
    numerator, totals = (
        lax.all_gather(numer_share, "seq", axis=2, tiled=True),
        lax.all_gather(total_share, "seq", axis=2, tiled=True),
    )
    attended = to_half(numerator / totals[..., None]).reshape(clip_count, latent_count, D)
    result = product("cnd,de->cne", attended, out_w)
    return (
        result,
        (
            residual,
            tokens,
            latent_normed,
            token_normed,
            queries,
            keyval,
            numerator,
            totals,
            attended,
        ),
    )


def cross_back(stored, grad_in, valid_keys, qkv_w, out_w, scales, offsets):
    residual, tokens, latent_normed, token_normed, queries, keyval, numerator, totals, attended = (
        stored
    )
    clip_count, latent_count, local_len = (residual.shape[0], residual.shape[1], tokens.shape[1])
    grad_a = to_half(grad_in)
    grad_out_w = product("cnd,cne->de", attended, grad_a)
    grad_att = (
        to_half(product("cne,de->cnd", grad_a, out_w))
        .reshape(clip_count, latent_count, HEADS, HEAD)
        .astype(jnp.float32)
    )
    grad_numer = to_half(grad_att / totals[..., None])
    grad_totals = -jnp.sum(grad_att * numerator, -1) / (totals * totals)
    weights_exp = cross_scores(queries, keyval[0], valid_keys)
    grad_weights = product("cqhd,ckhd->cqhk", grad_numer, keyval[1]) + grad_totals[..., None]
    grad_scores = to_half(weights_exp * grad_weights)
    grad_values = to_half(product("cqhk,cqhd->ckhd", to_half(weights_exp), grad_numer))
    grad_keys = to_half(product("cqhk,cqhd->ckhd", grad_scores, queries) * 0.125)
    grad_query_part = product("cqhk,ckhd->cqhd", grad_scores, keyval[0]) * 0.125
    query_share = lax.psum_scatter(
        grad_query_part.astype(jnp.bfloat16), "seq", scatter_dimension=2, tiled=True
    ).astype(jnp.float32)
    grad_queries = lax.all_gather(to_half(query_share), "seq", axis=2, tiled=True).reshape(
        clip_count, latent_count, D
    )
    grad_kv = jnp.stack([grad_keys, grad_values]).reshape(2, clip_count, local_len, D)
    grad_q_w = product("cnd,cne->de", latent_normed, grad_queries)
    grad_kv_w = product("cld,jcle->jde", token_normed, grad_kv)
    grad_latent_norm = product("cne,de->cnd", grad_queries, qkv_w[0])
    grad_token_norm = product("jcle,jde->cld", grad_kv, qkv_w[1:3])
    grad_rows, grad_scale_lat, grad_shift_lat = norm_back(
        residual, scales[0], offsets[0], grad_latent_norm
    )
    grad_tokens, grad_scale_tok, grad_shift_tok = norm_back(
        tokens, scales[1], offsets[1], grad_token_norm
    )
    grad_qkv = jnp.concatenate([grad_q_w[None], grad_kv_w])
    return (
        grad_rows,
        grad_tokens,
        (
            grad_qkv,
            grad_out_w,
            jnp.stack([grad_scale_lat, grad_scale_tok]),
            jnp.stack([grad_shift_lat, grad_shift_tok]),
        ),
    )


def per_device(
    latents_in,
    inputs,
    clip_frames,
    text_mask,
    qkv_weight,
    out_weight,
    mlp_in,
    mlp_out,
    norm_gain,
    norm_bias,
    bias_in,
    bias_out,
    out_cotangent,
):
    local_len = inputs.shape[2]
    seq_start = lax.axis_index("seq") * local_len
    positions = jnp.arange(FRAMES * PATCHES, dtype=jnp.int32)
    grad_sum = None
    finals = []
    latent_grads = []
    token_grads = []
    for micro_step in range(latents_in.shape[0]):
        gathered = (
            lax.all_gather(qkv_weight, "fsdp", axis=2, tiled=True),
            lax.all_gather(out_weight, "fsdp", axis=1, tiled=True),
            lax.all_gather(mlp_in, "fsdp", axis=1, tiled=True),
            lax.all_gather(mlp_out, "fsdp", axis=1, tiled=True),
            lax.all_gather(norm_gain, "fsdp", axis=1, tiled=True),
            lax.all_gather(norm_bias, "fsdp", axis=1, tiled=True),
            lax.all_gather(bias_in, "fsdp", axis=1, tiled=True),
            lax.all_gather(bias_out, "fsdp", axis=1, tiled=True),
        )
        qkv_w, out_w, up_w, down_w, gain_w, shift_w, up_bias, down_bias = gathered
        scales = gain_w.astype(jnp.float32)
        offsets = shift_w.astype(jnp.float32)
        up_b32 = up_bias.astype(jnp.float32)
        down_b32 = down_bias.astype(jnp.float32)
        frames_now = clip_frames[micro_step]
        full_mask = jnp.concatenate(
            [positions[None, :] < frames_now[:, None] * PATCHES, text_mask[micro_step] > 0], axis=1
        )
        valid_keys = lax.dynamic_slice_in_dim(full_mask, seq_start, local_len, 1)
        start_rows = latents_in[micro_step].astype(jnp.float32)
        token_rows = inputs[micro_step].astype(jnp.float32)
        cross_out, cross_saved = cross_forward(
            start_rows, token_rows, valid_keys, qkv_w[0], out_w[0], scales, offsets
        )
        first = start_rows + cross_out
        ff_one, ff_one_saved = feed_forward(
            first, up_w[0], down_w[0], up_b32[0], down_b32[0], scales[2], offsets[2]
        )
        second = first + ff_one
        self_out, self_saved = self_forward(second, qkv_w[1], out_w[1], scales[3], offsets[3])
        third = second + self_out
        ff_two, ff_two_saved = feed_forward(
            third, up_w[1], down_w[1], up_b32[1], down_b32[1], scales[4], offsets[4]
        )
        finals.append(third + ff_two)
        gathered = (
            lax.all_gather(qkv_weight, "fsdp", axis=2, tiled=True),
            lax.all_gather(out_weight, "fsdp", axis=1, tiled=True),
            lax.all_gather(mlp_in, "fsdp", axis=1, tiled=True),
            lax.all_gather(mlp_out, "fsdp", axis=1, tiled=True),
            lax.all_gather(norm_gain, "fsdp", axis=1, tiled=True),
            lax.all_gather(norm_bias, "fsdp", axis=1, tiled=True),
            lax.all_gather(bias_in, "fsdp", axis=1, tiled=True),
            lax.all_gather(bias_out, "fsdp", axis=1, tiled=True),
        )
        qkv_w, out_w, up_w, down_w, gain_w, shift_w, up_bias, down_bias = gathered
        scales = gain_w.astype(jnp.float32)
        offsets = shift_w.astype(jnp.float32)
        grad_four = out_cotangent[micro_step].astype(jnp.float32)
        grad_three, ff_two_grads = feed_back(
            ff_two_saved, grad_four, up_w[1], down_w[1], scales[4], offsets[4]
        )
        grad_three = grad_three + grad_four
        grad_two, self_grads = self_back(
            self_saved, grad_three, qkv_w[1], out_w[1], scales[3], offsets[3]
        )
        grad_two = grad_two + grad_three
        grad_one, ff_one_grads = feed_back(
            ff_one_saved, grad_two, up_w[0], down_w[0], scales[2], offsets[2]
        )
        grad_one = grad_one + grad_two
        grad_start, grad_tokens, cross_grads = cross_back(
            cross_saved, grad_one, valid_keys, qkv_w[0], out_w[0], scales, offsets
        )
        latent_grads.append(grad_start + grad_one)
        token_grads.append(grad_tokens)
        grad_qkv_all = jnp.stack([cross_grads[0], self_grads[0]])
        grad_out_all = jnp.stack([cross_grads[1], self_grads[1]])
        grad_up_all = jnp.stack([ff_one_grads[0], ff_two_grads[0]])
        grad_down_all = jnp.stack([ff_one_grads[1], ff_two_grads[1]])
        grad_gain_all = jnp.concatenate(
            [cross_grads[2], jnp.stack([ff_one_grads[4], self_grads[2], ff_two_grads[4]])]
        )
        grad_shift_all = jnp.concatenate(
            [cross_grads[3], jnp.stack([ff_one_grads[5], self_grads[3], ff_two_grads[5]])]
        )
        grad_upb_all = jnp.stack([ff_one_grads[2], ff_two_grads[2]])
        grad_downb_all = jnp.stack([ff_one_grads[3], ff_two_grads[3]])
        grad_step = (
            grad_qkv_all,
            grad_out_all,
            grad_up_all,
            grad_down_all,
            grad_gain_all,
            grad_shift_all,
            grad_upb_all,
            grad_downb_all,
        )
        grad_sum = grad_step if grad_sum is None else jax.tree.map(jnp.add, grad_sum, grad_step)
    grad_sum = (
        lax.psum_scatter(grad_sum[0], "fsdp", scatter_dimension=2, tiled=True),
        lax.psum_scatter(grad_sum[1], "fsdp", scatter_dimension=1, tiled=True),
        lax.psum_scatter(grad_sum[2], "fsdp", scatter_dimension=1, tiled=True),
        lax.psum_scatter(grad_sum[3], "fsdp", scatter_dimension=1, tiled=True),
        lax.psum_scatter(grad_sum[4], "fsdp", scatter_dimension=1, tiled=True),
        lax.psum_scatter(grad_sum[5], "fsdp", scatter_dimension=1, tiled=True),
        lax.psum_scatter(grad_sum[6], "fsdp", scatter_dimension=1, tiled=True),
        lax.psum_scatter(grad_sum[7], "fsdp", scatter_dimension=1, tiled=True),
    )
    kv_part, gain_part, shift_part = (
        lax.psum(grad_sum[0][0, 1:3].astype(jnp.bfloat16), "seq").astype(jnp.float32),
        lax.psum(grad_sum[4][1].astype(jnp.bfloat16), "seq").astype(jnp.float32),
        lax.psum(grad_sum[5][1].astype(jnp.bfloat16), "seq").astype(jnp.float32),
    )
    qkv_final = grad_sum[0].at[0, 1:3].set(kv_part)
    gain_final = grad_sum[4].at[1].set(gain_part)
    shift_final = grad_sum[5].at[1].set(shift_part)
    return (
        jnp.stack(finals),
        jnp.stack(latent_grads),
        jnp.stack(token_grads),
        qkv_final,
        grad_sum[1],
        grad_sum[2],
        grad_sum[3],
        gain_final,
        shift_final,
        grad_sum[6],
        grad_sum[7],
    )


def solution(mesh):
    in_specs = (
        P(None, "fsdp", None, None),
        P(None, "fsdp", "seq", None),
        P(None, "fsdp"),
        P(None, "fsdp", None),
        P(None, None, "fsdp", None),
        P(None, "fsdp", None),
        P(None, "fsdp", None),
        P(None, "fsdp", None),
        P(None, "fsdp"),
        P(None, "fsdp"),
        P(None, "fsdp"),
        P(None, "fsdp"),
        P(None, "fsdp", None, None),
    )
    out_specs = (
        P(None, "fsdp", None, None),
        P(None, "fsdp", None, None),
        P(None, "fsdp", "seq", None),
        P(None, None, "fsdp", None),
        P(None, "fsdp", None),
        P(None, "fsdp", None),
        P(None, "fsdp", None),
        P(None, "fsdp"),
        P(None, "fsdp"),
        P(None, "fsdp"),
        P(None, "fsdp"),
    )
    return jax.shard_map(
        per_device, mesh=mesh, in_specs=in_specs, out_specs=out_specs, check_vma=False
    )
```

profile of v0, /device:TPU:0, one launch (start us, length us, event | category | flops | bytes accessed | tf_op | source)
XLA Modules:
  0.0 1272.3 jit_solution(13977146467657318002)
XLA Ops:
  8.0 10.5 all-gather.1
  18.5 8.8 all-gather
  32.8 10.1 fusion.290
  46.0 15.5 %all-gather.8.cloned.1.call-done = bf16[2,3,768,768]{3,2,1,0:T(8,128)(2,1)} async-done(((bf16[2,3,96,768]{3,2,1,0:T(8,128)(2,1)}), bf16[2,3,768,768]{3,2,1,0:T(8,128)(2,1)}) %all-gather.8.cloned.1.call-update) | async-done | bytes 7077904 | tf_op jit(solution)/shard_map/all_gather | solution.py:214
  130.3 8.7 all-gather.2
  140.4 8.0 all_gather.67
  149.6 18.7 %all-reduce.3 = (f32[1,128,12]{1,0,2:T(1,128)S(1)}, f32[1,128,12]{1,0,2:T(1,128)S(1)}) all-reduce(f32[1,128,12]{1,0,2:T(1,128)S(1)} %reduce_sum.702, f32[1,128,12]{1,0,2:T(1,128)S(1)} %reduce_sum.680), channel_id=5, replica_groups=mesh['fsdp'=8,'seq'=4] {'seq'}, use_global_device_ids=true, to_apply=%region_21.22.clone | all-reduce | flops 3072 | bytes 24576
  168.2 11.8 all_gather.71
  180.1 11.9 all_gather.64
  192.0 15.4 %all_gather.70 = f32[1,128,12,64]{1,3,0,2:T(8,128)S(1)} all-gather(f32[1,128,3,64]{1,3,0,2:T(8,128)} %bitcast.876), channel_id=1, replica_groups=mesh['fsdp'=8,'seq'=4] {'seq'}, dimensions={2}, use_global_device_ids=true | all-gather | bytes 491520 | tf_op jit(solution)/shard_map/all_gather | solution.py:119
  210.2 14.8 %all_gather.31 = f32[1,128,12,64]{1,3,0,2:T(8,128)S(1)} all-gather(f32[1,128,3,64]{1,3,0,2:T(8,128)} %bitcast.877), channel_id=1, replica_groups=mesh['fsdp'=8,'seq'=4] {'seq'}, dimensions={2}, use_global_device_ids=true | all-gather | bytes 491520 | tf_op jit(solution)/shard_map/all_gather | solution.py:119
  233.5 52.4 %all-gather.14.cloned.1.call-done = bf16[2,3072,768]{2,1,0:T(8,128)(2,1)} async-done(((bf16[2,384,768]{2,1,0:T(8,128)(2,1)}), bf16[2,3072,768]{2,1,0:T(8,128)(2,1)}) %all-gather.14.cloned.1.call-update) | async-done | bytes 9437200 | tf_op jit(solution)/shard_map/all_gather | solution.py:217
  392.7 7.5 convolution_convert_fusion
  423.8 7.5 convolution_convert_fusion.1
  464.1 10.5 fusion.75
  490.4 14.1 %all_gather.73 = bf16[1,128,12,64]{1,3,0,2:T(8,128)(2,1)S(1)} all-gather(bf16[1,128,3,64]{1,3,0,2:T(8,128)(2,1)} %bitcast.889), channel_id=1, replica_groups=mesh['fsdp'=8,'seq'=4] {'seq'}, dimensions={2}, use_global_device_ids=true | all-gather | bytes 245760 | tf_op jit(solution)/shard_map/all_gather | solution.py:163
  504.5 14.1 %all_gather.72 = bf16[1,128,12,64]{1,3,0,2:T(8,128)(2,1)S(1)} all-gather(bf16[1,128,3,64]{1,3,0,2:T(8,128)(2,1)} %bitcast.890), channel_id=1, replica_groups=mesh['fsdp'=8,'seq'=4] {'seq'}, dimensions={2}, use_global_device_ids=true | all-gather | bytes 245760 | tf_op jit(solution)/shard_map/all_gather | solution.py:163
  531.6 9.0 maximum_add_fusion.2
  540.6 21.6 %copy.326 = f32[2,3,768,768]{3,0,1,2:T(2,128)} copy(f32[2,3,768,768]{2,3,1,0:T(8,128)} %maximum_add_fusion.2) | data formatting | bytes 28311552 | tf_op jit(solution)/shard_map/add | solution.py:302
  592.6 11.7 bitcast_reduce_fusion.3
  604.7 9.0 fusion.17
  634.1 117.9 %all-reduce.10.cloned.1.call-done = f32[2,3,768,768]{3,0,1,2:T(2,128)} async-done(((f32[2,3,768,768]{3,0,1,2:T(2,128)}), f32[2,3,768,768]{3,0,1,2:T(2,128)}) %all-reduce.10.cloned.1.call-update) | async-done | bytes 14155792
  773.7 11.3 maximum_add_fusion
  797.6 11.8 maximum_add_fusion.1
  810.0 8.2 add_bitcast_fusion.1
  821.3 53.8 %copy.327 = f32[2,1,1578,768]{3,1,2,0:T(1,128)} copy(f32[2,1,1578,768]{3,2,1,0:T(8,128)S(1)} %pad_maximum_fusion) | data formatting | bytes 19390464
  886.8 18.8 %reduce-scatter.36.cloned.1.call-done = f32[96,5]{1,0:T(8,128)} async-done(((f32[768,5]{1,0:T(8,128)}), f32[96,5]{1,0:T(8,128)}) %reduce-scatter.36.cloned.1.call-update) | async-done | bytes 1936
  906.5 11.7 all-reduce.4
  920.4 26.9 %all-reduce.8.cloned.1.call-done = bf16[1,2,96,768]{3,0,1,2:T(2,128)(2,1)} async-done(((bf16[1,2,96,768]{3,0,1,2:T(2,128)(2,1)}), bf16[1,2,96,768]{3,0,1,2:T(2,128)(2,1)}) %all-reduce.8.cloned.1.call-update) | async-done | bytes 294928 | tf_op jit(solution)/shard_map/psum | solution.py:314
  956.2 49.0 %reduce-scatter.28.cloned.1.call-done = f32[2,96,768]{2,1,0:T(8,128)} async-done(((f32[2,768,768]{2,1,0:T(8,128)}), f32[2,96,768]{2,1,0:T(8,128)}) %reduce-scatter.28.cloned.1.call-update) | async-done | bytes 589840 | tf_op jit(solution)/shard_map/reduce_scatter | solution.py:305
  1005.2 130.2 %reduce-scatter.30.cloned.1.call-done = f32[2,96,3072]{2,1,0:T(8,128)} async-done(((f32[2,768,3072]{2,1,0:T(8,128)}), f32[2,96,3072]{2,1,0:T(8,128)}) %reduce-scatter.30.cloned.1.call-update) | async-done | bytes 2359312 | tf_op jit(solution)/shard_map/reduce_scatter | solution.py:306
  1135.4 130.2 %reduce-scatter.32.cloned.1.call-done = f32[2,384,768]{2,1,0:T(8,128)} async-done(((f32[2,3072,768]{2,1,0:T(8,128)}), f32[2,384,768]{2,1,0:T(8,128)}) %reduce-scatter.32.cloned.1.call-update) | async-done | bytes 2359312 | tf_op jit(solution)/shard_map/reduce_scatter | solution.py:307
  (823 shorter events, 390.5 us)
Async XLA Ops:
  7.2 54.4 %all-gather.8.cloned.1.call-start = ((), (), s32[]{:S(2)}) async-start(), calls=%async_computation.11 | async-start | bytes 7962624 | tf_op jit(solution)/shard_map/all_gather | solution.py:214
  7.9 184.1 %reduce-scatter.22.cloned.1.call-start = ((), (), s32[]{:S(2)}) async-start(), calls=%async_computation.16 | async-start | bytes 491520 | tf_op jit(solution)/shard_map/reduce_scatter | solution.py:115
  30.2 56.1 %copy-start.157 = (pred[1578]{0:T(1024)(128)(4,1)}, pred[1578]{0:T(1024)(128)(4,1)S(1)}, u32[]{:S(2)}) copy-start(pred[1578]{0:T(1024)(128)(4,1)S(1)} %fusion.235) | copy-start | bytes 4738
  30.3 67.2 %copy-start.186 = (f32[768]{0:T(1024)}, f32[768]{0:T(1024)S(1)}, u32[]{:S(2)}) copy-start(f32[768]{0:T(1024)S(1)} %get-tuple-element.153) | copy-start | bytes 9220
  30.3 267.9 %copy-start.123 = (f32[768]{0:T(1024)}, f32[768]{0:T(1024)S(1)}, u32[]{:S(2)}) copy-start(f32[768]{0:T(1024)S(1)} %get-tuple-element.151) | copy-start | bytes 9220
  30.3 289.6 %copy-start.125 = (f32[768]{0:T(1024)}, f32[768]{0:T(1024)S(1)}, u32[]{:S(2)}) copy-start(f32[768]{0:T(1024)S(1)} %get-tuple-element.149) | copy-start | bytes 9220
  30.3 306.5 %copy-start.121 = (f32[768]{0:T(1024)}, f32[768]{0:T(1024)S(1)}, u32[]{:S(2)}) copy-start(f32[768]{0:T(1024)S(1)} %get-tuple-element.270) | copy-start | bytes 9220
  32.8 62.1 %copy-start.215 = (f32[128]{0:T(128)}, f32[128]{0:T(128)S(1)}, u32[]{:S(2)}) copy-start(f32[128]{0:T(128)S(1)} %get-tuple-element.140) | copy-start | bytes 1540
  92.8 115.4 %all-gather.10.cloned.1.call-start = ((), (), s32[]{:S(2)}) async-start(), calls=%async_computation.13 | async-start | bytes 2654208 | tf_op jit(solution)/shard_map/all_gather | solution.py:215
  93.5 116.7 %reduce-scatter.20.cloned.1.call-start = ((), (), s32[]{:S(2)}) async-start(), calls=%async_computation.12 | async-start | bytes 491520 | tf_op jit(solution)/shard_map/reduce_scatter | solution.py:115
  129.1 100.0 %all-gather.12.cloned.1.call-start = ((), (), s32[]{:S(2)}) async-start(), calls=%async_computation.14 | async-start | bytes 10616832 | tf_op jit(solution)/shard_map/all_gather | solution.py:216
  129.7 156.2 %all-gather.14.cloned.1.call-start = ((), (), s32[]{:S(2)}) async-start(), calls=%async_computation.15 | async-start | bytes 10616832 | tf_op jit(solution)/shard_map/all_gather | solution.py:217
  130.3 360.1 %reduce-scatter.26.cloned.1.call-start = ((), (), s32[]{:S(2)}) async-start(), calls=%async_computation.18 | async-start | bytes 245760 | tf_op jit(solution)/shard_map/reduce_scatter | solution.py:160
  149.6 79.5 %copy-start.146 = (f32[1,3072]{1,0:T(1,128)}, f32[1,3072]{1,0:T(1,128)S(1)}, u32[]{:S(2)}) copy-start(f32[1,3072]{1,0:T(1,128)S(1)} %get-tuple-element.199) | copy-start | bytes 36868
  210.0 75.9 %copy-start.19 = (f32[128,768]{1,0:T(8,128)}, f32[128,768]{1,0:T(8,128)S(1)}, u32[]{:S(2)}) copy-start(f32[128,768]{1,0:T(8,128)S(1)} %get-tuple-element.232) | copy-start | bytes 1179652
  227.6 70.6 %copy-start.150 = (f32[128]{0:T(128)}, f32[128]{0:T(128)S(1)}, u32[]{:S(2)}) copy-start(f32[128]{0:T(128)S(1)} %broadcast_multiply_fusion.8) | copy-start | bytes 1540
  229.1 56.8 %copy-start.188 = (f32[768]{0:T(1024)S(1)}, f32[768]{0:T(1024)}, u32[]{:S(2)}) copy-start(f32[768]{0:T(1024)} %get-tuple-element.155) | copy-start | bytes 9220
  416.0 88.4 %reduce-scatter.24.cloned.1.call-start = ((), (), s32[]{:S(2)}) async-start(), calls=%async_computation.17 | async-start | bytes 245760 | tf_op jit(solution)/shard_map/reduce_scatter | solution.py:160
  463.6 288.4 %all-reduce.10.cloned.1.call-start = ((), (), s32[]{:S(2)}) async-start(), calls=%async_computation.27 | async-start | bytes 28311552
  562.3 319.3 %reduce-scatter.40.cloned.1.call-start = ((), (), s32[]{:S(2)}) async-start(), calls=%async_computation.26 | async-start | bytes 442368
  604.4 278.6 %reduce-scatter.38.cloned.1.call-start = ((), (), s32[]{:S(2)}) async-start(), calls=%async_computation.25 | async-start | bytes 1769472
  617.7 268.3 %reduce-scatter.34.cloned.1.call-start = ((), (), s32[]{:S(2)}) async-start(), calls=%async_computation.23 | async-start | bytes 442368
  624.6 130.0 %copy-start.109 = (bf16[12,64,128]{2,1,0:T(8,128)(2,1)S(1)}, bf16[12,64,128]{2,1,0:T(8,128)(2,1)}, u32[]{:S(2)}) copy-start(bf16[12,64,128]{2,1,0:T(8,128)(2,1)} %copy-done.108) | copy-start | bytes 589828
  624.6 130.0 %copy-start.115 = (bf16[128,768]{1,0:T(8,128)(2,1)S(1)}, bf16[128,768]{1,0:T(8,128)(2,1)}, u32[]{:S(2)}) copy-start(bf16[128,768]{1,0:T(8,128)(2,1)} %copy-done.114) | copy-start | bytes 589828
  624.6 281.0 %reduce-scatter.36.cloned.1.call-start = ((), (), s32[]{:S(2)}) async-start(), calls=%async_computation.24 | async-start | bytes 442368
  634.1 313.2 %all-reduce.8.cloned.1.call-start = ((), (), s32[]{:S(2)}) async-start(), calls=%async_computation.19 | async-start | bytes 1179648 | tf_op jit(solution)/shard_map/psum | solution.py:314
  754.5 250.6 %reduce-scatter.28.cloned.1.call-start = ((), (), s32[]{:S(2)}) async-start(), calls=%async_computation.20 | async-start | bytes 5308416 | tf_op jit(solution)/shard_map/reduce_scatter | solution.py:305
  761.5 373.9 %reduce-scatter.30.cloned.1.call-start = ((), (), s32[]{:S(2)}) async-start(), calls=%async_computation.21 | async-start | bytes 21233664 | tf_op jit(solution)/shard_map/reduce_scatter | solution.py:306
  785.0 480.6 %reduce-scatter.32.cloned.1.call-start = ((), (), s32[]{:S(2)}) async-start(), calls=%async_computation.22 | async-start | bytes 21233664 | tf_op jit(solution)/shard_map/reduce_scatter | solution.py:307
  821.2 53.8 %copy-start.15 = (f32[128,768]{1,0:T(8,128)S(1)}, f32[128,768]{1,0:T(8,128)}, u32[]{:S(2)}) copy-start(f32[128,768]{1,0:T(8,128)} %copy-done.13) | copy-start | bytes 1179652
  821.3 57.4 %slice-start.12 = ((s8[9437184]{0:T(1024)(128)(4,1)}), s8[1048576]{0:T(1024)(128)(4,1)S(1)}, s32[]{:S(2)}) async-start(s8[9437184]{0:T(1024)(128)(4,1)} %bitcast.909), calls=%async_computation.40 | async-start | bytes 2097152
  821.3 57.4 %slice-start.13 = ((s8[9437184]{0:T(1024)(128)(4,1)}), s8[4194304]{0:T(1024)(128)(4,1)S(1)}, s32[]{:S(2)}) async-start(s8[9437184]{0:T(1024)(128)(4,1)} %bitcast.909), calls=%async_computation.41 | async-start | bytes 8388608
  (238 other events, 1616.6 us)
Sparse Core Ops, SparseCore 0:
  9.9 51.5 all-gather.7
  92.9 20.5 reduce-scatter.21
  115.6 27.2 all-gather.9
  145.7 20.6 reduce-scatter.19
  168.2 56.9 all-gather.11
  227.0 58.8 all-gather.13
  416.2 19.3 reduce-scatter.25
  463.7 19.4 reduce-scatter.23
  562.4 189.5 all-reduce.9
  755.2 33.9 reduce-scatter.39
  792.9 38.4 reduce-scatter.37
  834.6 33.7 reduce-scatter.33
  871.7 33.8 reduce-scatter.35
  908.0 39.3 all-reduce.7
  951.6 53.5 reduce-scatter.27
  1009.2 126.1 reduce-scatter.29
  1139.4 126.1 reduce-scatter.31
where the time goes:
time: 1280 us; the launch traced here: 1270 us
  waiting for transfers between devices  544 us (42%)
  matrix products  246 us (19%)
  local copies, waits for them, and re-layouts  220 us (17%)
  blocking collectives  148 us (12%)
  other arithmetic  91.5 us (7%)
  between operations  20.5 us (2%)
    dot_general x78, matrix products, product(): return jnp.einsum(form, left, right, preferred_element_type=jnp.float32)  246 us
    unnamed x22, waiting for transfers between devices  139 us
    reduce_scatter x1, waiting for transfers between devices, per_device(): lax.psum_scatter(grad_sum[2], 'fsdp', scatter_dimension=1, tiled=True)  130 us
    reduce_scatter x1, waiting for transfers between devices, per_device(): lax.psum_scatter(grad_sum[3], 'fsdp', scatter_dimension=1, tiled=True)  130 us
    unnamed x525, local copies, waits for them, and re-layouts  90.3 us
    all_gather x1, waiting for transfers between devices, per_device(): lax.all_gather(mlp_out, 'fsdp', axis=1, tiled=True)  52.4 us
    reduce_scatter x1, waiting for transfers between devices, per_device(): lax.psum_scatter(grad_sum[1], 'fsdp', scatter_dimension=1, tiled=True)  49 us
    add x8, other arithmetic, per_device(): jax.tree.map(jnp.add, grad_sum, grad_step)  37.3 us
  transfers between devices with their start and end apart: 17, of which 8 were waited for; matrix products, arithmetic and copies ran while one was open for 27% of the time, Pallas kernels for 0%

commit v1 on v0

--- a/solution.py
+++ b/solution.py
@@ -9,6 +9,19 @@
 PATCHES = 392
 FRAMES = 16
 epsilon = 1e-06
+
+
+def gather_around(x, axis, dim):
+    ways = lax.axis_size(axis)
+    up = [(d, (d + 1) % ways) for d in range(ways)]
+    down = [(d, (d - 1) % ways) for d in range(ways)]
+    earlier, later = ([x], [x])
+    for _ in range(ways // 2):
+        earlier.append(lax.ppermute(earlier[-1], axis, up))
+    for _ in range((ways - 1) // 2):
+        later.append(lax.ppermute(later[-1], axis, down))
+    line = jnp.concatenate([*earlier[::-1], *later[1:]], axis=dim)
+    return jnp.roll(line, (lax.axis_index(axis) - ways // 2) * x.shape[dim], axis=dim)
 
 
 def layer_norm(values, scales, offsets):
@@ -214,7 +227,7 @@
             lax.all_gather(qkv_weight, "fsdp", axis=2, tiled=True),
             lax.all_gather(out_weight, "fsdp", axis=1, tiled=True),
             lax.all_gather(mlp_in, "fsdp", axis=1, tiled=True),
-            lax.all_gather(mlp_out, "fsdp", axis=1, tiled=True),
+            gather_around(mlp_out, "fsdp", 1),
             lax.all_gather(norm_gain, "fsdp", axis=1, tiled=True),
             lax.all_gather(norm_bias, "fsdp", axis=1, tiled=True),
             lax.all_gather(bias_in, "fsdp", axis=1, tiled=True),

time: 1280 us -> 1380 us (1.078)
  waiting for transfers between devices: 544 us -> 587 us
  other arithmetic: 91.5 us -> 113 us
  blocking collectives: 148 us -> 166 us
  starting transfers between devices: 2.18 us -> 18.9 us
    ppermute x0 -> x7, waiting for transfers between devices: none -> 105 us  [the longest x4 90.9 us: gather_around(): earlier.append(lax.ppermute(earlier[-1], axis, up))]
    all_gather x1, waiting for transfers between devices: 52.4 us -> 0.01 us  [per_device(): lax.all_gather(mlp_out, 'fsdp', axis=1, tiled=True)]
    all_gather x1, blocking collectives: 8.7 us -> 26.4 us  [per_device(): lax.all_gather(bias_out, 'fsdp', axis=1, tiled=True)]
    unnamed x525 -> x626, local copies, waits for them, and re-layouts: 90.3 us -> 96 us
  transfers between devices with their start and end apart: 17 -> 24, of which waited for: 8 -> 12; matrix products, arithmetic and copies ran while one was open for 27% -> 29% of each run, Pallas kernels for 0% -> 0%
where the time goes in v1:
time: 1380 us; the launch traced here: 1370 us
  waiting for transfers between devices  587 us (43%)
  matrix products  241 us (17%)
  local copies, waits for them, and re-layouts  225 us (16%)
  blocking collectives  166 us (12%)
  other arithmetic  113 us (8%)
  between operations  21.1 us (2%)
  starting transfers between devices  18.9 us (1%)
    dot_general x78, matrix products, product(): return jnp.einsum(form, left, right, preferred_element_type=jnp.float32)  241 us
    unnamed x22, waiting for transfers between devices  130 us
    reduce_scatter x1, waiting for transfers between devices, per_device(): lax.psum_scatter(grad_sum[2], 'fsdp', scatter_dimension=1, tiled=True)  130 us
    reduce_scatter x1, waiting for transfers between devices, per_device(): lax.psum_scatter(grad_sum[3], 'fsdp', scatter_dimension=1, tiled=True)  130 us
    unnamed x626, local copies, waits for them, and re-layouts  96 us
    ppermute x4, waiting for transfers between devices, gather_around(): earlier.append(lax.ppermute(earlier[-1], axis, up))  90.9 us
    reduce_scatter x1, waiting for transfers between devices, per_device(): lax.psum_scatter(grad_sum[1], 'fsdp', scatter_dimension=1, tiled=True)  49.1 us
    add x8, other arithmetic, per_device(): jax.tree.map(jnp.add, grad_sum, grad_step)  39.7 us
  transfers between devices with their start and end apart: 24, of which 12 were waited for; matrix products, arithmetic and copies ran while one was open for 29% of the time, Pallas kernels for 0%

profile of v1, /device:TPU:0, one launch (start us, length us, event | category | flops | bytes accessed | tf_op | source)
XLA Modules:
  0.0 1372.6 jit_solution(9944563871698447671)
XLA Ops:
  8.0 10.5 all-gather.1
  32.9 10.2 fusion.291
  46.2 15.4 %all-gather.8.cloned.1.call-done = bf16[2,3,768,768]{3,2,1,0:T(8,128)(2,1)} async-done(((bf16[2,3,96,768]{3,2,1,0:T(8,128)(2,1)}), bf16[2,3,768,768]{3,2,1,0:T(8,128)(2,1)}) %all-gather.8.cloned.1.call-update) | async-done | bytes 7077904 | tf_op jit(solution)/shard_map/all_gather | solution.py:227
  91.5 10.3 reduce-scatter.20.cloned.1.call-start
  134.1 18.9 %collective-permute-done = bf16[2,384,768]{2,1,0:T(8,128)(2,1)} collective-permute-done((bf16[2,384,768]{2,1,0:T(8,128)(2,1)S(1)}, bf16[2,384,768]{2,1,0:T(8,128)(2,1)}, u32[]{:S(2)}, u32[]{:S(2)}) %collective-permute-start) | collective-permute-done | bytes 1179680 | tf_op jit(solution)/shard_map/ppermute | solution.py:20
  155.6 31.3 %collective-permute-done.1 = bf16[2,384,768]{2,1,0:T(8,128)(2,1)S(1)} collective-permute-done((bf16[2,384,768]{2,1,0:T(8,128)(2,1)}, bf16[2,384,768]{2,1,0:T(8,128)(2,1)S(1)}, u32[]{:S(2)}, u32[]{:S(2)}) %collective-permute-start.1) | collective-permute-done | bytes 1179680 | tf_op jit(solution)/shard_map/ppermute | solution.py:20
  191.5 40.7 %collective-permute-done.2 = bf16[2,384,768]{2,1,0:T(8,128)(2,1)} collective-permute-done((bf16[2,384,768]{2,1,0:T(8,128)(2,1)S(1)}, bf16[2,384,768]{2,1,0:T(8,128)(2,1)}, u32[]{:S(2)}, u32[]{:S(2)}) %collective-permute-start.2) | collective-permute-done | bytes 1179680 | tf_op jit(solution)/shard_map/ppermute | solution.py:20
  232.2 26.4 %all-gather.2 = bf16[8,96,2]{1,2,0:T(2,128)(2,1)S(1)} all-gather(bf16[1,96,2]{1,2,0:T(2,128)(2,1)S(1)} %bitcast.912), channel_id=1, replica_groups=mesh['fsdp'=8,'seq'=4] {'fsdp'}, dimensions={0}, use_global_device_ids=true | all-gather | bytes 3456 | tf_op jit(solution)/shard_map/all_gather | solution.py:234
  276.4 12.1 collective-permute-done.6
  289.9 12.0 fusion.4
  301.8 18.9 %all-reduce.3 = (f32[1,128,12]{1,0,2:T(1,128)S(1)}, f32[1,128,12]{1,0,2:T(1,128)S(1)}) all-reduce(f32[1,128,12]{1,0,2:T(1,128)S(1)} %reduce_sum.702, f32[1,128,12]{1,0,2:T(1,128)S(1)} %reduce_sum.680), channel_id=5, replica_groups=mesh['fsdp'=8,'seq'=4] {'seq'}, use_global_device_ids=true, to_apply=%region_21.23.clone | all-reduce | flops 3072 | bytes 24576
  320.8 11.8 all_gather.68
  333.2 11.9 all_gather.62
  345.1 15.4 %all_gather.67 = f32[1,128,12,64]{1,3,0,2:T(8,128)S(1)} all-gather(f32[1,128,3,64]{1,3,0,2:T(8,128)} %bitcast.884), channel_id=1, replica_groups=mesh['fsdp'=8,'seq'=4] {'seq'}, dimensions={2}, use_global_device_ids=true | all-gather | bytes 491520 | tf_op jit(solution)/shard_map/all_gather | solution.py:132
  363.4 15.0 %all_gather.61 = f32[1,128,12,64]{1,3,0,2:T(8,128)S(1)} all-gather(f32[1,128,3,64]{1,3,0,2:T(8,128)} %bitcast.885), channel_id=1, replica_groups=mesh['fsdp'=8,'seq'=4] {'seq'}, dimensions={2}, use_global_device_ids=true | all-gather | bytes 491520 | tf_op jit(solution)/shard_map/all_gather | solution.py:132
  564.8 10.4 fusion.76
  591.1 13.9 %all_gather.71 = bf16[1,128,12,64]{1,3,0,2:T(8,128)(2,1)S(1)} all-gather(bf16[1,128,3,64]{1,3,0,2:T(8,128)(2,1)} %bitcast.897), channel_id=1, replica_groups=mesh['fsdp'=8,'seq'=4] {'seq'}, dimensions={2}, use_global_device_ids=true | all-gather | bytes 245760 | tf_op jit(solution)/shard_map/all_gather | solution.py:176
  604.9 13.9 %all_gather.70 = bf16[1,128,12,64]{1,3,0,2:T(8,128)(2,1)S(1)} all-gather(bf16[1,128,3,64]{1,3,0,2:T(8,128)(2,1)} %bitcast.898), channel_id=1, replica_groups=mesh['fsdp'=8,'seq'=4] {'seq'}, dimensions={2}, use_global_device_ids=true | all-gather | bytes 245760 | tf_op jit(solution)/shard_map/all_gather | solution.py:176
  632.3 10.6 maximum_add_fusion.2
  642.9 21.7 %copy.326 = f32[2,3,768,768]{3,0,1,2:T(2,128)} copy(f32[2,3,768,768]{2,3,1,0:T(8,128)} %maximum_add_fusion.2) | data formatting | bytes 28311552 | tf_op jit(solution)/shard_map/add | solution.py:315
  694.6 11.6 bitcast_reduce_fusion.3
  740.4 112.0 %all-reduce.10.cloned.1.call-done = f32[2,3,768,768]{3,0,1,2:T(2,128)} async-done(((f32[2,3,768,768]{3,0,1,2:T(2,128)}), f32[2,3,768,768]{3,0,1,2:T(2,128)}) %all-reduce.10.cloned.1.call-update) | async-done | bytes 14155792
  873.6 11.4 maximum_add_fusion
  896.7 11.8 maximum_add_fusion.1
  909.2 10.5 add_bitcast_fusion.1
  924.2 53.8 %copy.327 = f32[2,1,1578,768]{3,1,2,0:T(1,128)} copy(f32[2,1,1578,768]{3,2,1,0:T(8,128)S(1)} %pad_maximum_fusion) | data formatting | bytes 19390464
  989.8 16.1 %reduce-scatter.36.cloned.1.call-done = f32[96,5]{1,0:T(8,128)} async-done(((f32[768,5]{1,0:T(8,128)}), f32[96,5]{1,0:T(8,128)}) %reduce-scatter.36.cloned.1.call-update) | async-done | bytes 1936
  1006.8 11.7 all-reduce.4
  1020.7 26.9 %all-reduce.8.cloned.1.call-done = bf16[1,2,96,768]{3,0,1,2:T(2,128)(2,1)} async-done(((bf16[1,2,96,768]{3,0,1,2:T(2,128)(2,1)}), bf16[1,2,96,768]{3,0,1,2:T(2,128)(2,1)}) %all-reduce.8.cloned.1.call-update) | async-done | bytes 294928 | tf_op jit(solution)/shard_map/psum | solution.py:327
  1056.4 49.1 %reduce-scatter.28.cloned.1.call-done = f32[2,96,768]{2,1,0:T(8,128)} async-done(((f32[2,768,768]{2,1,0:T(8,128)}), f32[2,96,768]{2,1,0:T(8,128)}) %reduce-scatter.28.cloned.1.call-update) | async-done | bytes 589840 | tf_op jit(solution)/shard_map/reduce_scatter | solution.py:318
  1105.5 130.2 %reduce-scatter.30.cloned.1.call-done = f32[2,96,3072]{2,1,0:T(8,128)} async-done(((f32[2,768,3072]{2,1,0:T(8,128)}), f32[2,96,3072]{2,1,0:T(8,128)}) %reduce-scatter.30.cloned.1.call-update) | async-done | bytes 2359312 | tf_op jit(solution)/shard_map/reduce_scatter | solution.py:319
  1235.7 130.2 %reduce-scatter.32.cloned.1.call-done = f32[2,384,768]{2,1,0:T(8,128)} async-done(((f32[2,3072,768]{2,1,0:T(8,128)}), f32[2,384,768]{2,1,0:T(8,128)}) %reduce-scatter.32.cloned.1.call-update) | async-done | bytes 2359312 | tf_op jit(solution)/shard_map/reduce_scatter | solution.py:320
  (941 shorter events, 445.2 us)
Async XLA Ops:
  7.2 54.4 %all-gather.8.cloned.1.call-start = ((), (), s32[]{:S(2)}) async-start(), calls=%async_computation.11 | async-start | bytes 7962624 | tf_op jit(solution)/shard_map/all_gather | solution.py:227
  7.9 337.2 %reduce-scatter.22.cloned.1.call-start = ((), (), s32[]{:S(2)}) async-start(), calls=%async_computation.15 | async-start | bytes 491520 | tf_op jit(solution)/shard_map/reduce_scatter | solution.py:128
  30.3 360.8 %copy-start.124 = (f32[768]{0:T(1024)}, f32[768]{0:T(1024)S(1)}, u32[]{:S(2)}) copy-start(f32[768]{0:T(1024)S(1)} %get-tuple-element.152) | copy-start | bytes 9220
  30.3 368.6 %copy-start.152 = (f32[768]{0:T(1024)}, f32[768]{0:T(1024)S(1)}, u32[]{:S(2)}) copy-start(f32[768]{0:T(1024)S(1)} %get-tuple-element.270) | copy-start | bytes 9220
  30.3 368.6 %copy-start.159 = (f32[768]{0:T(1024)}, f32[768]{0:T(1024)S(1)}, u32[]{:S(2)}) copy-start(f32[768]{0:T(1024)S(1)} %get-tuple-element.151) | copy-start | bytes 9220
  30.3 385.6 %copy-start.126 = (f32[768]{0:T(1024)}, f32[768]{0:T(1024)S(1)}, u32[]{:S(2)}) copy-start(f32[768]{0:T(1024)S(1)} %get-tuple-element.150) | copy-start | bytes 9220
  30.4 404.1 %copy-start.122 = (f32[768]{0:T(1024)}, f32[768]{0:T(1024)S(1)}, u32[]{:S(2)}) copy-start(f32[768]{0:T(1024)S(1)} %get-tuple-element.271) | copy-start | bytes 9220
  90.8 270.6 %all-gather.10.cloned.1.call-start = ((), (), s32[]{:S(2)}) async-start(), calls=%async_computation.13 | async-start | bytes 2654208 | tf_op jit(solution)/shard_map/all_gather | solution.py:228
  91.5 271.9 %reduce-scatter.20.cloned.1.call-start = ((), (), s32[]{:S(2)}) async-start(), calls=%async_computation.12 | async-start | bytes 491520 | tf_op jit(solution)/shard_map/reduce_scatter | solution.py:128
  130.0 128.6 %copy-start.254 = (bf16[2,384]{1,0:T(2,128)(2,1)S(1)}, bf16[2,384]{1,0:T(2,128)(2,1)}, u32[]{:S(2)}) copy-start(bf16[2,384]{1,0:T(2,128)(2,1)} %param.31) | copy-start | bytes 4612
  130.0 138.9 %copy-start.276 = (u32[32]{0:T(128)S(1)}, u32[32]{0:T(128)}, u32[]{:S(2)}) copy-start(u32[32]{0:T(128)} %constant.192) | copy-start | bytes 388
  132.8 248.5 %all-gather.12.cloned.1.call-start = ((), (), s32[]{:S(2)}) async-start(), calls=%async_computation.14 | async-start | bytes 10616832 | tf_op jit(solution)/shard_map/all_gather | solution.py:229
  133.4 284.6 %all-gather.14.cloned.1.call-start = ((), (), s32[]{:S(2)}) async-start(), calls=%async_computation.16 | async-start | bytes 10616832 | tf_op jit(solution)/shard_map/all_gather | solution.py:266
  133.5 19.4 %collective-permute-start = (bf16[2,384,768]{2,1,0:T(8,128)(2,1)S(1)}, bf16[2,384,768]{2,1,0:T(8,128)(2,1)}, u32[]{:S(2)}, u32[]{:S(2)}) collective-permute-start(bf16[2,384,768]{2,1,0:T(8,128)(2,1)S(1)} %copy-done.46), channel_id=1, source_target_pairs={{0,4},{4,8},{8,12},{12,16},{16,20},{20,24},{24,28},{28,0},{1,5},{5... | collective-permute-start | bytes 3538952 | tf_op jit(solution)/shard_map/ppermute | solution.py:20
  134.0 457.0 %reduce-scatter.26.cloned.1.call-start = ((), (), s32[]{:S(2)}) async-start(), calls=%async_computation.18 | async-start | bytes 245760 | tf_op jit(solution)/shard_map/reduce_scatter | solution.py:173
  152.9 34.0 %collective-permute-start.1 = (bf16[2,384,768]{2,1,0:T(8,128)(2,1)}, bf16[2,384,768]{2,1,0:T(8,128)(2,1)S(1)}, u32[]{:S(2)}, u32[]{:S(2)}) collective-permute-start(bf16[2,384,768]{2,1,0:T(8,128)(2,1)} %collective-permute-done), channel_id=1, source_target_pairs={{0,4},{4,8},{8,12},{12,16},{16,20},{20,24},{24,28},{28,0},{1,5},{5... | collective-permute-start | bytes 3538952 | tf_op jit(solution)/shard_map/ppermute | solution.py:20
  152.9 35.7 %collective-permute-start.4 = (bf16[2,384,768]{2,1,0:T(8,128)(2,1)S(1)}, bf16[2,384,768]{2,1,0:T(8,128)(2,1)S(1)}, u32[]{:S(2)}, u32[]{:S(2)}) collective-permute-start(bf16[2,384,768]{2,1,0:T(8,128)(2,1)S(1)} %copy-done.47), channel_id=1, source_target_pairs={{0,28},{4,0},{8,4},{12,8},{16,12},{20,16},{24,20},{28,24},{1,29},{... | collective-permute-start | bytes 3538952 | tf_op jit(solution)/shard_map/ppermute | solution.py:22
  186.9 45.3 %collective-permute-start.2 = (bf16[2,384,768]{2,1,0:T(8,128)(2,1)S(1)}, bf16[2,384,768]{2,1,0:T(8,128)(2,1)}, u32[]{:S(2)}, u32[]{:S(2)}) collective-permute-start(bf16[2,384,768]{2,1,0:T(8,128)(2,1)S(1)} %collective-permute-done.1), channel_id=1, source_target_pairs={{0,4},{4,8},{8,12},{12,16},{16,20},{20,24},{24,28},{28,0},{1,5},{5... | collective-permute-start | bytes 3538952 | tf_op jit(solution)/shard_map/ppermute | solution.py:20
  188.6 78.8 %collective-permute-start.5 = (bf16[2,384,768]{2,1,0:T(8,128)(2,1)S(1)}, bf16[2,384,768]{2,1,0:T(8,128)(2,1)}, u32[]{:S(2)}, u32[]{:S(2)}) collective-permute-start(bf16[2,384,768]{2,1,0:T(8,128)(2,1)S(1)} %collective-permute-done.4), channel_id=1, source_target_pairs={{0,28},{4,0},{8,4},{12,8},{16,12},{20,16},{24,20},{28,24},{1,29},{... | collective-permute-start | bytes 3538952 | tf_op jit(solution)/shard_map/ppermute | solution.py:22
  232.2 38.6 %collective-permute-start.3 = (bf16[2,384,768]{2,1,0:T(8,128)(2,1)}, bf16[2,384,768]{2,1,0:T(8,128)(2,1)}, u32[]{:S(2)}, u32[]{:S(2)}) collective-permute-start(bf16[2,384,768]{2,1,0:T(8,128)(2,1)} %collective-permute-done.2), channel_id=1, source_target_pairs={{0,4},{4,8},{8,12},{12,16},{16,20},{20,24},{24,28},{28,0},{1,5},{5... | collective-permute-start | bytes 3538952 | tf_op jit(solution)/shard_map/ppermute | solution.py:20
  267.4 21.1 %collective-permute-start.6 = (bf16[2,384,768]{2,1,0:T(8,128)(2,1)}, bf16[2,384,768]{2,1,0:T(8,128)(2,1)}, u32[]{:S(2)}, u32[]{:S(2)}) collective-permute-start(bf16[2,384,768]{2,1,0:T(8,128)(2,1)} %collective-permute-done.5), channel_id=1, source_target_pairs={{0,28},{4,0},{8,4},{12,8},{16,12},{20,16},{24,20},{28,24},{1,29},{... | collective-permute-start | bytes 3538952 | tf_op jit(solution)/shard_map/ppermute | solution.py:22
  516.7 88.2 %reduce-scatter.24.cloned.1.call-start = ((), (), s32[]{:S(2)}) async-start(), calls=%async_computation.17 | async-start | bytes 245760 | tf_op jit(solution)/shard_map/reduce_scatter | solution.py:173
  564.5 287.9 %all-reduce.10.cloned.1.call-start = ((), (), s32[]{:S(2)}) async-start(), calls=%async_computation.27 | async-start | bytes 28311552
  664.6 319.9 %reduce-scatter.40.cloned.1.call-start = ((), (), s32[]{:S(2)}) async-start(), calls=%async_computation.26 | async-start | bytes 442368
  706.2 279.7 %reduce-scatter.38.cloned.1.call-start = ((), (), s32[]{:S(2)}) async-start(), calls=%async_computation.25 | async-start | bytes 1769472
  722.8 266.2 %reduce-scatter.34.cloned.1.call-start = ((), (), s32[]{:S(2)}) async-start(), calls=%async_computation.23 | async-start | bytes 442368
  724.6 130.3 %copy-start.110 = (bf16[12,64,128]{2,1,0:T(8,128)(2,1)S(1)}, bf16[12,64,128]{2,1,0:T(8,128)(2,1)}, u32[]{:S(2)}) copy-start(bf16[12,64,128]{2,1,0:T(8,128)(2,1)} %copy-done.109) | copy-start | bytes 589828
  729.6 276.3 %reduce-scatter.36.cloned.1.call-start = ((), (), s32[]{:S(2)}) async-start(), calls=%async_computation.24 | async-start | bytes 442368
  740.3 307.3 %all-reduce.8.cloned.1.call-start = ((), (), s32[]{:S(2)}) async-start(), calls=%async_computation.19 | async-start | bytes 1179648 | tf_op jit(solution)/shard_map/psum | solution.py:327
  854.9 250.6 %reduce-scatter.28.cloned.1.call-start = ((), (), s32[]{:S(2)}) async-start(), calls=%async_computation.20 | async-start | bytes 5308416 | tf_op jit(solution)/shard_map/reduce_scatter | solution.py:318
  861.4 374.3 %reduce-scatter.30.cloned.1.call-start = ((), (), s32[]{:S(2)}) async-start(), calls=%async_computation.21 | async-start | bytes 21233664 | tf_op jit(solution)/shard_map/reduce_scatter | solution.py:319
  884.9 480.9 %reduce-scatter.32.cloned.1.call-start = ((), (), s32[]{:S(2)}) async-start(), calls=%async_computation.22 | async-start | bytes 21233664 | tf_op jit(solution)/shard_map/reduce_scatter | solution.py:320
  (292 other events, 3101.2 us)
Sparse Core Ops, SparseCore 0:
  9.9 51.5 all-gather.7
  90.9 20.5 reduce-scatter.21
  113.6 28.3 all-gather.9
  144.8 20.9 reduce-scatter.19
  167.5 82.7 all-gather.11
  252.1 73.9 all-gather.13
  516.8 17.4 reduce-scatter.25
  564.6 17.4 reduce-scatter.23
  664.7 187.5 all-reduce.9
  855.6 33.9 reduce-scatter.39
  893.2 38.4 reduce-scatter.37
  934.9 33.7 reduce-scatter.33
  972.1 33.8 reduce-scatter.35
  1008.2 39.3 all-reduce.7
  1051.9 53.5 reduce-scatter.27
  1109.5 126.1 reduce-scatter.29
  1239.7 126.1 reduce-scatter.31
